TPU v7x, 32 devices: a whole 2x2x4 slice. The times are simulated.
32 devices in a mesh: tp: 4 (over y, x), rep: 8 (over z, core).
Axes of the slice: x: 2, y: 2, z: 4, core: 2. Of those that a mesh axis runs over, the one named last changes fastest.
Arguments:
- queries: bfloat16 [128, 4096], P('rep', 'tp'), may hold values from -6 to 6
- new_keys: bfloat16 [128, 2048], P('rep', 'tp'), may hold values from -6 to 6
- new_values: bfloat16 [128, 2048], P('rep', 'tp'), may hold values from -6 to 6
- stored_keys: bfloat16 [128, 16, 128, 128], P('rep', 'tp'), may hold values from -6 to 6
- stored_values: bfloat16 [128, 16, 128, 128], P('rep', 'tp'), may hold values from -6 to 6
- lengths: int32 [128], P('rep'), may hold values from 1 to 128
- out_proj: bfloat16 [4096, 4608], P('tp', 'rep'), may hold values from -0.09375 to 0.09375
- residual: bfloat16 [128, 4608], P(None, 'rep'), may hold values from -4.5 to 4.5
- norm_gain: float32 [4608], replicated, may hold values from 0.1 to 1.9
- embedding: bfloat16 [256000, 4608], P(('tp', 'rep')), may hold values from -1.25 to 1.25
- targets: int32 [128], replicated, may hold values from 0 to 255999
- old_sums: float32 [128], P('rep'), may hold values from -3 to 0
- rewards: float32 [128], P('rep'), may hold values from -6 to 6
- group_ids: int32 [128], P('rep'), may hold values from 0 to 15, as said below
Outputs:
- logprob_sum: float32 [128], P('rep')
- advantage: float32 [128], P('rep')
Inputs may be any that keep to these rules, and one draw needn't show every extreme that they name: `group_ids`: each id names exactly 8 continuations.
All inputs are finite; a program needn't handle non-finite values.
Results may differ from a plain program's by a relative error of at most 0.001.
Values may be sent and summed in bfloat16 or wider, within the bound.
A program may use at most 128 MiB of HBM per device.

v0:
```python
import jax
import jax.numpy as jnp
from jax import lax
from jax.sharding import PartitionSpec as P

GROUP = 8


def attention(queries, new_keys, new_values, stored_keys, stored_values, lengths):
    samp, heads_kv, span, depth = stored_keys.shape
    sample_ratio = queries.shape[1] // (heads_kv * depth)
    query_vector = queries.reshape(samp, heads_kv, sample_ratio, depth)
    scores = (
        jnp.einsum("sgqd,sgpd->sgqp", query_vector, stored_keys, preferred_element_type=jnp.float32)
        / 12.0
    )
    scores = 50.0 * jnp.tanh(scores / 50.0)
    valid = lax.broadcasted_iota(jnp.int32, (samp, 1, 1, span), 3) < lengths[:, None, None, None]
    expo = jnp.where(valid, jnp.exp(scores), 0.0)
    own_logit = (
        jnp.einsum(
            "sgqd,sgd->sgq",
            query_vector,
            new_keys.reshape(samp, heads_kv, depth),
            preferred_element_type=jnp.float32,
        )
        / 12.0
    )
    own_logit = 50.0 * jnp.tanh(own_logit / 50.0)
    own_exp = jnp.exp(own_logit)
    total = jnp.sum(expo, -1) + own_exp
    probs = (expo / total[..., None]).astype(jnp.bfloat16)
    own_probability = (own_exp / total).astype(jnp.bfloat16)
    attended_output = jnp.einsum(
        "sgqp,sgpd->sgqd", probs, stored_values, preferred_element_type=jnp.float32
    )
    attended_output = attended_output + own_probability.astype(jnp.float32)[
        ..., None
    ] * new_values.reshape(samp, heads_kv, 1, depth).astype(jnp.float32)
    return attended_output.reshape(samp, sample_ratio * heads_kv * depth).astype(jnp.bfloat16)


def per_device(
    queries,
    new_keys,
    new_values,
    stored_keys,
    stored_values,
    lengths,
    out_proj,
    residual,
    norm_gain,
    embedding,
    targets,
    old_sums,
    rewards,
    group_ids,
):
    samp = queries.shape[0]
    reps = lax.axis_size("rep")
    rep_index = lax.axis_index("rep")
    tp_index = lax.axis_index("tp")
    groups = samp * reps // GROUP
    member = group_ids[:, None] == lax.broadcasted_iota(jnp.int32, (1, groups), 1)
    reward_part = jnp.sum(jnp.where(member, rewards[:, None], 0.0), 0)
    group_total = lax.psum(reward_part, "rep")
    mine = jnp.sum(jnp.where(member, group_total[None, :], 0.0), 1)
    advantage = rewards - (mine - rewards) / (GROUP - 1.0)
    context = attention(queries, new_keys, new_values, stored_keys, stored_values, lengths)
    partial_value = jnp.dot(
        lax.all_gather(context, "rep", axis=0, tiled=True),
        out_proj,
        preferred_element_type=jnp.float32,
    )
    vocab_rows = embedding.shape[0]
    contract = (((1,), (1,)), ((), ()))
    heads = lax.psum(partial_value, "tp")
    stream = residual.astype(jnp.float32) + heads
    full = lax.all_gather(stream, "rep", axis=1, tiled=True)
    scale = lax.rsqrt(jnp.mean(full * full, axis=1, keepdims=True) + 1e-06)
    normed = (full * scale * norm_gain[None, :]).astype(jnp.bfloat16)
    logits = lax.dot_general(normed, embedding, contract, preferred_element_type=jnp.float32)
    capped = 30.0 * jnp.tanh(logits / 30.0)
    offset = (tp_index * reps + rep_index) * vocab_rows
    entry_ids = offset + lax.broadcasted_iota(jnp.int32, (1, vocab_rows), 1)
    picked_part = jnp.sum(jnp.where(entry_ids == targets[:, None], capped, 0.0), 1)
    total, picked = lax.psum((jnp.sum(jnp.exp(capped), 1), picked_part), ("tp", "rep"))
    logprob = picked - jnp.log(total)
    own_rows = lax.dynamic_slice_in_dim(logprob, rep_index * samp, samp)
    logprob_sum = old_sums + own_rows
    return (logprob_sum, advantage)


def solution(mesh):
    in_specs = (
        P("rep", "tp"),
        P("rep", "tp"),
        P("rep", "tp"),
        P("rep", "tp", None, None),
        P("rep", "tp", None, None),
        P("rep"),
        P("tp", "rep"),
        P(None, "rep"),
        P(),
        P(("tp", "rep"), None),
        P(),
        P("rep"),
        P("rep"),
        P("rep"),
    )
    out_specs = (P("rep"), P("rep"))
    return jax.shard_map(
        per_device, mesh=mesh, in_specs=in_specs, out_specs=out_specs, check_vma=False
    )
```

profile of v0, /device:TPU:0, one launch (start us, length us, event | category | flops | bytes accessed | tf_op | source)
XLA Modules:
  0.0 191.0 jit_solution(11185303319291343823)
XLA Ops:
  7.2 0.9 reshape.60
  8.2 0.7 iota_compare_fusion.1
  8.9 1.3 fusion.15
  10.2 0.1 copy.18
  10.3 0.8 reshape.66
  11.1 0.2 fusion.16
  11.3 0.1 copy.22
  11.4 0.1 copy.19
  11.6 0.1 copy.20
  11.7 0.6 reshape.62
  12.3 2.9 %fusion.8 = bf16[16,4,2,128]{3,2,1,0:T(2,128)(2,1)} fusion(bf16[16,4,128,128]{3,2,1,0:T(8,128)(2,1)} %param.18, f32[16,4,2,128]{3,2,1,0:T(2,128)S(1)} %get-tuple-element.9, f32[16,4,128]{2,1,0:T(4,128)} %reshape.62, f32[16,4,2]{2,1,0:T(4,128)S(1)} %copy.20, f32[16,4,2]{2,1,0:T(4,128)S(1)} %copy.19), kind=kOutput, calls=%fused_computation.15 | convolution fusion | flops 4276224 | bytes 2229248 | tf_op jit(solution)/shard_map/sgqp,sgpd->sgqd/dot_general | solution.py:34
  15.2 0.8 convert_element_type.39
  16.1 15.9 %all_gather.6 = bf16[128,1024]{1,0:T(8,128)(2,1)S(1)} all-gather(bf16[16,1024]{1,0:T(8,128)(2,1)S(1)} %convert_element_type.39), channel_id=1, replica_groups=mesh['tp'=4,'rep'=8] {'rep'}, dimensions={0}, use_global_device_ids=true | all-gather | bytes 294912 | tf_op jit(solution)/shard_map/all_gather | solution.py:71
  32.0 1.2 fusion.17
  33.2 44.5 %all-reduce.3.cloned.1.call-done = f32[128,576]{0,1:T(8,128)} async-done(((f32[128,576]{0,1:T(8,128)}), f32[128,576]{0,1:T(8,128)}) %all-reduce.3.cloned.1.call-update) | async-done | bytes 294928 | tf_op jit(solution)/shard_map/psum | solution.py:77
  77.7 1.7 convert_add_fusion
  79.6 16.4 %psum.31 = f32[16]{0:T(128)S(1)} all-reduce(f32[16]{0:T(128)S(1)} %select_reduce_fusion.2), channel_id=1, replica_groups=mesh['tp'=4,'rep'=8] {'rep'}, use_global_device_ids=true, to_apply=%region_8.9 | all-reduce | flops 16 | bytes 128 | tf_op jit(solution)/shard_map/psum | solution.py:66
  96.0 0.2 select_reduce_fusion.1
  96.2 0.5 multiply_subtract_fusion
  96.7 14.5 %all-gather.2.cloned.1.call-done = f32[128,4608]{0,1:T(8,128)} async-done(((f32[128,576]{0,1:T(8,128)}), f32[128,4608]{0,1:T(8,128)}) %all-gather.2.cloned.1.call-update) | async-done | bytes 2359312 | tf_op jit(solution)/shard_map/all_gather | solution.py:79
  111.2 2.4 %multiply_reduce_fusion = f32[128]{0:T(128)S(1)} fusion(f32[128,4608]{0,1:T(8,128)} %all-gather.2.cloned.1.call-done), kind=kLoop, calls=%fused_computation.6 | loop fusion | flops 1179520 | bytes 2359808 | tf_op jit(solution)/shard_map/reduce_sum | solution.py:80
  113.7 30.2 %exponential_reduce_fusion = (f32[128]{0:T(128)S(1)}, f32[128]{0:T(128)S(1)}) fusion(s32[128]{0:T(128)S(1)} %copy-done.9, s32[8000]{0:T(1024)S(1)} %iota_add_fusion, bf16[8000,4608]{1,0:T(8,128)(2,1)} %param.23, f32[128,4608]{0,1:T(8,128)S(1)} %copy-done.1, f32[4608]{0:T(1024)S(1)} %copy-done.6, f32[128]{0:T(128)S(1)} %add_rsqrt_fusion), kind=kOutput, calls=%fused_computation.3 | convolution fusion | flops 9445097472 | bytes 76139776 | tf_op jit(solution)/shard_map/dot_general | solution.py:82
  143.8 39.7 %all-reduce = (f32[128]{0:T(128)S(1)}, f32[128]{0:T(128)S(1)}) all-reduce(f32[128]{0:T(128)S(1)} %get-tuple-element.3, f32[128]{0:T(128)S(1)} %get-tuple-element.2), channel_id=1, replica_groups=mesh['tp'=4,'rep'=8] {'tp','rep'}, use_global_device_ids=true, to_apply=%region_4.5 | all-reduce | flops 256 | bytes 2048 | tf_op jit(solution)/shard_map/psum | solution.py:87
  183.6 0.6 dynamic-slice_add_fusion
  (29 shorter events, 0.3 us)
Async XLA Ops:
  7.2 1.7 copy-start
  7.2 4.5 %copy-start.4 = (bf16[16,512]{1,0:T(8,128)(2,1)S(1)}, bf16[16,512]{1,0:T(8,128)(2,1)}, u32[]{:S(2)}) copy-start(bf16[16,512]{1,0:T(8,128)(2,1)} %param.16) | copy-start | bytes 49156
  7.2 70.5 %all-reduce.3.cloned.1.call-start = ((), (), s32[]{:S(2)}) async-start(), calls=%async_computation | async-start | bytes 589824 | tf_op jit(solution)/shard_map/psum | solution.py:77
  10.2 21.8 %copy-start.2 = (bf16[1024,576]{0,1:T(8,128)(2,1)S(1)}, bf16[1024,576]{0,1:T(8,128)(2,1)}, u32[]{:S(2)}) copy-start(bf16[1024,576]{0,1:T(8,128)(2,1)} %param.20) | copy-start | bytes 3538948
  12.3 65.4 %copy-start.3 = (bf16[128,576]{0,1:T(8,128)(2,1)S(1)}, bf16[128,576]{0,1:T(8,128)(2,1)}, u32[]{:S(2)}) copy-start(bf16[128,576]{0,1:T(8,128)(2,1)} %param.21) | copy-start | bytes 442372
  15.2 64.2 %copy-start.7 = (s32[16]{0:T(128)S(1)}, s32[16]{0:T(128)}, u32[]{:S(2)}) copy-start(s32[16]{0:T(128)} %param.27) | copy-start | bytes 196
  15.2 64.2 %copy-start.8 = (f32[16]{0:T(128)S(1)}, f32[16]{0:T(128)}, u32[]{:S(2)}) copy-start(f32[16]{0:T(128)} %param.26) | copy-start | bytes 196
  32.0 81.7 %copy-start.6 = (f32[4608]{0:T(1024)S(1)}, f32[4608]{0:T(1024)}, u32[]{:S(2)}) copy-start(f32[4608]{0:T(1024)} %param.22) | copy-start | bytes 55300
  32.0 81.7 %copy-start.9 = (s32[128]{0:T(128)S(1)}, s32[128]{0:T(128)}, u32[]{:S(2)}) copy-start(s32[128]{0:T(128)} %param.24) | copy-start | bytes 1540
  33.2 78.0 %all-gather.2.cloned.1.call-start = ((), (), s32[]{:S(2)}) async-start(), calls=%async_computation.1 | async-start | bytes 2654208 | tf_op jit(solution)/shard_map/all_gather | solution.py:79
  111.2 2.5 %copy-start.1 = (f32[128,4608]{0,1:T(8,128)S(1)}, f32[128,4608]{0,1:T(8,128)}, u32[]{:S(2)}) copy-start(f32[128,4608]{0,1:T(8,128)} %all-gather.2.cloned.1.call-done) | copy-start | bytes 7077892
  113.7 69.9 %copy-start.5 = (f32[16]{0:T(128)S(1)}, f32[16]{0:T(128)}, u32[]{:S(2)}) copy-start(f32[16]{0:T(128)} %param.25) | copy-start | bytes 196
Sparse Core Ops, SparseCore 0:
  33.3 44.3 all-reduce.2
  79.6 31.5 all-gather.1
where the time goes:
time: 191 us
  blocking collectives  72.1 us (38%)
  waiting for transfers between devices  59 us (31%)
  matrix products  35.8 us (19%)
  between operations  14.1 us (7%)
  other arithmetic  6.3 us (3%)
  local copies, waits for them, and re-layouts  3.63 us (2%)
    psum x1, waiting for transfers between devices, per_device(): heads = lax.psum(partial_value, 'tp')  44.5 us
    psum x1, blocking collectives, per_device(): lax.psum((jnp.sum(jnp.exp(capped), 1), picked_part), ('tp', 'rep'))  39.7 us
    dot_general x1, matrix products, per_device(): lax.dot_general(normed, embedding, contract, preferred_element_type=jnp.f...  30.2 us
    psum x1, blocking collectives, per_device(): group_total = lax.psum(reward_part, 'rep')  16.4 us
    all_gather x1, blocking collectives, per_device(): lax.all_gather(context, 'rep', axis=0, tiled=True)  15.9 us
    all_gather x1, waiting for transfers between devices, per_device(): full = lax.all_gather(stream, 'rep', axis=1, tiled=True)  14.5 us
  transfers between devices with their start and end apart: 2, of which 2 were waited for; matrix products, arithmetic and copies ran while one was open for 0% of the time, Pallas kernels for 0%

commit v1 on v0

--- a/solution.py
+++ b/solution.py
@@ -4,6 +4,12 @@
 from jax.sharding import PartitionSpec as P
 
 GROUP = 8
+
+
+def mark_figure_for(matrix, axis_name, mesh_name):
+    for h in (axis_name, mesh_name):
+        matrix = lax.psum(matrix, h)
+    return matrix
 
 
 def attention(queries, new_keys, new_values, stored_keys, stored_values, lengths):
@@ -84,7 +90,7 @@
     offset = (tp_index * reps + rep_index) * vocab_rows
     entry_ids = offset + lax.broadcasted_iota(jnp.int32, (1, vocab_rows), 1)
     picked_part = jnp.sum(jnp.where(entry_ids == targets[:, None], capped, 0.0), 1)
-    total, picked = lax.psum((jnp.sum(jnp.exp(capped), 1), picked_part), ("tp", "rep"))
+    total, picked = mark_figure_for((jnp.sum(jnp.exp(capped), 1), picked_part), "rep", "tp")
     logprob = picked - jnp.log(total)
     own_rows = lax.dynamic_slice_in_dim(logprob, rep_index * samp, samp)
     logprob_sum = old_sums + own_rows

time: 191 us -> 177 us (0.927)
  blocking collectives: 72.1 us -> 40.8 us
  waiting for transfers between devices: 59 us -> 76 us
    psum x2, blocking collectives: 56.1 us -> 24.9 us  [mark_figure_for(): matrix = lax.psum(matrix, h)]
    all_gather x1, waiting for transfers between devices: 14.5 us -> 31.5 us  [per_device(): full = lax.all_gather(stream, 'rep', axis=1, tiled=True)]
where the time goes in v1:
time: 177 us
  waiting for transfers between devices  76 us (43%)
  blocking collectives  40.8 us (23%)
  matrix products  35.8 us (20%)
  between operations  14.1 us (8%)
  other arithmetic  6.3 us (4%)
  local copies, waits for them, and re-layouts  3.63 us (2%)
    psum x1, waiting for transfers between devices, per_device(): heads = lax.psum(partial_value, 'tp')  44.5 us
    all_gather x1, waiting for transfers between devices, per_device(): full = lax.all_gather(stream, 'rep', axis=1, tiled=True)  31.5 us
    dot_general x1, matrix products, per_device(): lax.dot_general(normed, embedding, contract, preferred_element_type=jnp.f...  30.2 us
    psum x2, blocking collectives, mark_figure_for(): matrix = lax.psum(matrix, h)  24.9 us
    all_gather x1, blocking collectives, per_device(): lax.all_gather(context, 'rep', axis=0, tiled=True)  15.9 us
  transfers between devices with their start and end apart: 2, of which 2 were waited for; matrix products, arithmetic and copies ran while one was open for 0% of the time, Pallas kernels for 0%

profile of v1, /device:TPU:0, one launch (start us, length us, event | category | flops | bytes accessed | tf_op | source)
XLA Modules:
  0.0 176.7 jit_solution(15862483424096703027)
XLA Ops:
  7.2 0.9 reshape.60
  8.2 0.7 iota_compare_fusion.1
  8.9 1.3 fusion.15
  10.2 0.1 copy.18
  10.3 0.8 reshape.66
  11.1 0.2 fusion.16
  11.3 0.1 copy.22
  11.4 0.1 copy.19
  11.6 0.1 copy.20
  11.7 0.6 reshape.62
  12.3 2.9 %fusion.8 = bf16[16,4,2,128]{3,2,1,0:T(2,128)(2,1)} fusion(bf16[16,4,128,128]{3,2,1,0:T(8,128)(2,1)} %param.18, f32[16,4,2,128]{3,2,1,0:T(2,128)S(1)} %get-tuple-element.12, f32[16,4,128]{2,1,0:T(4,128)} %reshape.62, f32[16,4,2]{2,1,0:T(4,128)S(1)} %copy.20, f32[16,4,2]{2,1,0:T(4,128)S(1)} %copy.19), kind=kOutput, calls=%fused_computation.15 | convolution fusion | flops 4276224 | bytes 2229248 | tf_op jit(solution)/shard_map/sgqp,sgpd->sgqd/dot_general | solution.py:40
  15.2 0.8 convert_element_type.39
  16.1 15.9 %all_gather.6 = bf16[128,1024]{1,0:T(8,128)(2,1)S(1)} all-gather(bf16[16,1024]{1,0:T(8,128)(2,1)S(1)} %convert_element_type.39), channel_id=1, replica_groups=mesh['tp'=4,'rep'=8] {'rep'}, dimensions={0}, use_global_device_ids=true | all-gather | bytes 294912 | tf_op jit(solution)/shard_map/all_gather | solution.py:77
  32.0 1.2 fusion.17
  33.2 44.5 %all-reduce.4.cloned.1.call-done = f32[128,576]{0,1:T(8,128)} async-done(((f32[128,576]{0,1:T(8,128)}), f32[128,576]{0,1:T(8,128)}) %all-reduce.4.cloned.1.call-update) | async-done | bytes 294928 | tf_op jit(solution)/shard_map/psum | solution.py:83
  77.7 1.7 convert_add_fusion
  79.6 31.5 %all-gather.2.cloned.1.call-done = f32[128,4608]{0,1:T(8,128)} async-done(((f32[128,576]{0,1:T(8,128)}), f32[128,4608]{0,1:T(8,128)}) %all-gather.2.cloned.1.call-update) | async-done | bytes 2359312 | tf_op jit(solution)/shard_map/all_gather | solution.py:85
  111.1 2.4 %multiply_reduce_fusion = f32[128]{0:T(128)S(1)} fusion(f32[128,4608]{0,1:T(8,128)} %all-gather.2.cloned.1.call-done), kind=kLoop, calls=%fused_computation.6 | loop fusion | flops 1179520 | bytes 2359808 | tf_op jit(solution)/shard_map/reduce_sum | solution.py:86
  113.5 30.2 %exponential_reduce_fusion = (f32[128]{0:T(128)S(1)}, f32[128]{0:T(128)S(1)}) fusion(s32[128]{0:T(128)S(1)} %copy-done.7, s32[8000]{0:T(1024)S(1)} %iota_add_fusion, bf16[8000,4608]{1,0:T(8,128)(2,1)} %param.23, f32[128,4608]{0,1:T(8,128)S(1)} %copy-done.1, f32[4608]{0:T(1024)S(1)} %copy-done.6, f32[128]{0:T(128)S(1)} %add_rsqrt_fusion), kind=kOutput, calls=%fused_computation.3 | convolution fusion | flops 9445097472 | bytes 76139776 | tf_op jit(solution)/shard_map/dot_general | solution.py:88
  143.7 15.1 %all-reduce = (f32[128]{0:T(128)S(1)}, f32[128]{0:T(128)S(1)}, f32[16]{0:T(128)S(1)}) all-reduce(f32[128]{0:T(128)S(1)} %get-tuple-element.3, f32[128]{0:T(128)S(1)} %get-tuple-element.2, f32[16]{0:T(128)S(1)} %select_reduce_fusion.2), channel_id=1, replica_groups=mesh['tp'=4,'rep'=8] {'rep'}, use_global_device_ids=true, to_apply=%region_4.5 | all-reduce | flops 272 | bytes 2176 | tf_op jit(solution)/shard_map/psum | solution.py:11
  158.8 0.2 select_reduce_fusion.1
  159.0 0.5 multiply_subtract_fusion
  159.5 9.8 %all-reduce.1 = (f32[128]{0:T(128)S(1)}, f32[128]{0:T(128)S(1)}) all-reduce(f32[128]{0:T(128)S(1)} %get-tuple-element.4, f32[128]{0:T(128)S(1)} %get-tuple-element.5), channel_id=1, replica_groups=mesh['tp'=4,'rep'=8] {'tp'}, use_global_device_ids=true, to_apply=%region_5.6 | all-reduce | flops 256 | bytes 2048 | tf_op jit(solution)/shard_map/psum | solution.py:11
  169.3 0.6 dynamic-slice_add_fusion
  (29 shorter events, 0.3 us)
Async XLA Ops:
  7.2 1.7 copy-start
  7.2 4.5 %copy-start.4 = (bf16[16,512]{1,0:T(8,128)(2,1)S(1)}, bf16[16,512]{1,0:T(8,128)(2,1)}, u32[]{:S(2)}) copy-start(bf16[16,512]{1,0:T(8,128)(2,1)} %param.16) | copy-start | bytes 49156
  7.2 70.5 %all-reduce.4.cloned.1.call-start = ((), (), s32[]{:S(2)}) async-start(), calls=%async_computation | async-start | bytes 589824 | tf_op jit(solution)/shard_map/psum | solution.py:83
  10.2 21.8 %copy-start.2 = (bf16[1024,576]{0,1:T(8,128)(2,1)S(1)}, bf16[1024,576]{0,1:T(8,128)(2,1)}, u32[]{:S(2)}) copy-start(bf16[1024,576]{0,1:T(8,128)(2,1)} %param.20) | copy-start | bytes 3538948
  12.3 65.4 %copy-start.3 = (bf16[128,576]{0,1:T(8,128)(2,1)S(1)}, bf16[128,576]{0,1:T(8,128)(2,1)}, u32[]{:S(2)}) copy-start(bf16[128,576]{0,1:T(8,128)(2,1)} %param.21) | copy-start | bytes 442372
  15.2 64.2 %copy-start.8 = (s32[16]{0:T(128)S(1)}, s32[16]{0:T(128)}, u32[]{:S(2)}) copy-start(s32[16]{0:T(128)} %param.27) | copy-start | bytes 196
  15.2 64.2 %copy-start.9 = (f32[16]{0:T(128)S(1)}, f32[16]{0:T(128)}, u32[]{:S(2)}) copy-start(f32[16]{0:T(128)} %param.26) | copy-start | bytes 196
  32.0 81.5 %copy-start.6 = (f32[4608]{0:T(1024)S(1)}, f32[4608]{0:T(1024)}, u32[]{:S(2)}) copy-start(f32[4608]{0:T(1024)} %param.22) | copy-start | bytes 55300
  32.0 81.5 %copy-start.7 = (s32[128]{0:T(128)S(1)}, s32[128]{0:T(128)}, u32[]{:S(2)}) copy-start(s32[128]{0:T(128)} %param.24) | copy-start | bytes 1540
  33.2 77.9 %all-gather.2.cloned.1.call-start = ((), (), s32[]{:S(2)}) async-start(), calls=%async_computation.1 | async-start | bytes 2654208 | tf_op jit(solution)/shard_map/all_gather | solution.py:85
  111.1 2.5 %copy-start.1 = (f32[128,4608]{0,1:T(8,128)S(1)}, f32[128,4608]{0,1:T(8,128)}, u32[]{:S(2)}) copy-start(f32[128,4608]{0,1:T(8,128)} %all-gather.2.cloned.1.call-done) | copy-start | bytes 7077892
  113.5 55.8 %copy-start.5 = (f32[16]{0:T(128)S(1)}, f32[16]{0:T(128)}, u32[]{:S(2)}) copy-start(f32[16]{0:T(128)} %param.25) | copy-start | bytes 196
Sparse Core Ops, SparseCore 0:
  33.3 44.3 all-reduce.3
  79.6 31.4 all-gather.1
